TPU v7x, 32 devices: a whole 2x2x4 slice. The times are simulated.
32 devices in a mesh: dp: 16 (over z, y, x), mp: 2 (over core).
Axes of the slice: x: 2, y: 2, z: 4, core: 2. Of those that a mesh axis runs over, the one named last changes fastest.
Arguments:
- inputs: bfloat16 [32768, 4096], P('dp', 'mp'), may hold values from -6 to 6
- cotangents: bfloat16 [32768, 4096], P('dp', 'mp'), may hold values from -6 to 6
- loss_token_mask: int32 [32768], P('dp'), may hold values 0 or 1
- adapter_down_weight: bfloat16 [128, 4096], P(None, 'mp'), may hold values from -0.09375 to 0.09375
- adapter_up_weight: bfloat16 [4096, 128], P('mp'), may hold values from -0.5 to 0.5
- width_projection: bfloat16 [2, 4096, 256], P(None, 'mp'), may hold values from -0.09375 to 0.09375
- rank_projection: bfloat16 [2, 128, 16], replicated, may hold values from -0.5 to 0.5
- targets: float32 [64, 8192], P(None, ('dp', 'mp')), may hold values from -500 to 500
Outputs:
- scores: float32 [128, 64], P('dp')
All inputs are finite; a program needn't handle non-finite values. No bound on the sum of `loss_token_mask` on one device may be relied on, other than what follows from the above.
Results may differ from a plain program's by a relative error of at most 0.0003.
Values sent between devices are 32-bit elements; how exact they have to be, the bound alone decides.
A program may use at most 64 MiB of HBM per device.

v0:
```python
import math
import jax
import jax.numpy as jnp
from jax import lax
from jax.sharding import PartitionSpec as P

SEQ = 256
KP = 256
KQ = 16
FEAT = 8192
adapter_scale = 4.0
epsilon = 1e-06


def on_device(
    inputs,
    cotangents,
    loss_token_mask,
    adapter_down_weight,
    adapter_up_weight,
    width_projection,
    rank_projection,
    targets,
):
    samples = inputs.shape[0] // SEQ
    masked_gradient = cotangents * loss_token_mask.astype(jnp.bfloat16)[:, None]
    cols_first = rank_projection[0].astype(jnp.float32)
    cols_second = rank_projection[1].astype(jnp.float32)
    down_partial_gradient = jnp.dot(
        inputs, adapter_down_weight.T, preferred_element_type=jnp.float32
    )
    up_partial_gradient = jnp.dot(
        masked_gradient, adapter_up_weight, preferred_element_type=jnp.float32
    )
    down_rank_product, up_rank_product = lax.psum(
        (down_partial_gradient, up_partial_gradient), "mp"
    )
    compact_up_gradient = jnp.dot(up_rank_product, cols_first, precision=lax.Precision.HIGHEST)
    compact_down_gradient = jnp.dot(down_rank_product, cols_second, precision=lax.Precision.HIGHEST)
    projected_activations = jnp.dot(
        inputs, width_projection[0], preferred_element_type=jnp.float32
    ).reshape(samples, SEQ, KP)
    projected_masked_gradient = jnp.dot(
        masked_gradient, width_projection[1], preferred_element_type=jnp.float32
    ).reshape(samples, SEQ, KP)
    first_matrix = adapter_scale * jnp.einsum(
        "stk,stq->skq",
        projected_activations,
        compact_up_gradient.reshape(samples, SEQ, KQ),
        precision=lax.Precision.HIGHEST,
    )
    second_matrix = adapter_scale * jnp.einsum(
        "stk,stq->skq",
        projected_masked_gradient,
        compact_down_gradient.reshape(samples, SEQ, KQ),
        precision=lax.Precision.HIGHEST,
    )
    partial_value = jnp.concatenate(
        [first_matrix.reshape(samples, KP * KQ), second_matrix.reshape(samples, KP * KQ)], axis=1
    )
    features = lax.psum(partial_value, "mp")
    every_target = lax.all_gather(targets, ("dp", "mp"), axis=1, tiled=True)
    inner = jnp.dot(features, every_target.T, precision=lax.Precision.HIGHEST)
    sample_squares = jnp.sum(features * features, axis=1)
    target_squares = jnp.sum(every_target * every_target, axis=1)
    sample_rms = jnp.sqrt(sample_squares / FEAT + epsilon)
    target_rms = jnp.sqrt(target_squares / FEAT + epsilon)
    return inner / (math.sqrt(FEAT) * sample_rms[:, None] * target_rms[None, :])


def solution(mesh):
    in_specs = (
        P("dp", "mp"),
        P("dp", "mp"),
        P("dp"),
        P(None, "mp"),
        P("mp", None),
        P(None, "mp", None),
        P(),
        P(None, ("dp", "mp")),
    )
    out_specs = P("dp", None)
    return jax.shard_map(
        on_device, mesh=mesh, in_specs=in_specs, out_specs=out_specs, check_vma=False
    )
```

profile of v0, /device:TPU:0, one launch (start us, length us, event | category | flops | bytes accessed | tf_op | source)
XLA Modules:
  0.0 130.8 jit_solution(16499203396642434931)
XLA Ops:
  7.4 0.0 copy-start
  7.4 0.0 all-reduce.6.cloned.1.call-start
  7.4 0.8 convert_element_type.2
  8.1 7.2 %broadcast_multiply_fusion = bf16[2048,2048]{1,0:T(8,128)(2,1)} fusion(bf16[2048,2048]{1,0:T(8,128)(2,1)} %param.9, bf16[2048]{0:T(1024)(128)(2,1)S(1)} %convert_element_type.2), kind=kLoop, calls=%fused_computation | loop fusion | flops 4194304 | bytes 16781312 | tf_op jit(solution)/shard_map/mul | solution.py:26
  15.4 0.0 copy-done
  15.4 0.0 copy-start.1
  15.4 0.0 copy-start.7
  15.4 6.9 %fusion.13 = f32[2048,128]{1,0:T(8,128)} fusion(bf16[2048,2048]{1,0:T(8,128)(2,1)} %param.8, bf16[128,2048]{1,0:T(8,128)(2,1)S(1)} %copy-done), kind=kOutput, calls=%fused_computation.22 | convolution fusion | flops 1073741824 | bytes 9961472 | tf_op jit(solution)/shard_map/dot_general | solution.py:29
  22.2 0.0 copy-done.1
  22.2 0.0 copy-done.7
  22.3 3.4 %fusion.12 = f32[2048,128]{1,0:T(8,128)} fusion(bf16[2048,2048]{1,0:T(8,128)(2,1)S(1)} %copy-done.1, bf16[2048,128]{1,0:T(8,128)(2,1)S(1)} %copy-done.7), kind=kOutput, calls=%fused_computation.21 | convolution fusion | flops 1073741824 | bytes 9961472 | tf_op jit(solution)/shard_map/dot_general | solution.py:32
  25.7 0.0 all-reduce.6.cloned.1.call-update
  25.7 0.2 all-reduce.4.cloned.1.call-start
  25.9 0.0 copy-start.6
  25.9 6.1 %fusion = f32[8,256,256]{2,1,0:T(8,128)S(1)} fusion(bf16[8,256,2048]{2,1,0:T(8,128)(2,1)} %bitcast.34, bf16[2,2048,256]{2,1,0:T(8,128)(2,1)} %param.13), kind=kOutput, calls=%fused_computation.5 | convolution fusion | flops 2147483648 | bytes 11534336 | tf_op jit(solution)/shard_map/dot_general | solution.py:43
  32.0 0.0 copy-done.6
  32.1 0.0 copy-start.5
  32.1 7.8 %fusion.2 = f32[8,256,256]{2,1,0:T(8,128)} fusion(bf16[8,256,2048]{2,1,0:T(8,128)(2,1)} %bitcast.37, bf16[2,2048,256]{2,1,0:T(8,128)(2,1)S(1)} %copy-done.6), kind=kOutput, calls=%fused_computation.7 | convolution fusion | flops 2147483648 | bytes 11534336 | tf_op jit(solution)/shard_map/dot_general | solution.py:40
  39.9 10.0 %all-reduce.6.cloned.1.call-done = (f32[8,256,128]{2,1,0:T(8,128)}, f32[8,256,128]{2,1,0:T(8,128)}) async-done(((f32[8,256,128]{2,1,0:T(8,128)}, f32[8,256,128]{2,1,0:T(8,128)}), (f32[8,256,128]{2,1,0:T(8,128)}, f32[8,256,128]{2,1,0:T(8,128)})) %all-reduce.6.cloned.1.call-update) | async-done | bytes 2097168 | tf_op jit(solution)/shard_map/psum | solution.py:35
  49.8 0.0 copy-done.5
  49.8 1.8 %fusion.6 = f32[8,256,16]{1,2,0:T(8,128)S(1)} fusion(f32[8,256,128]{2,1,0:T(8,128)} %get-tuple-element.5, bf16[2,128,16]{1,2,0:T(8,128)(2,1)S(1)} %copy-done.5), kind=kOutput, calls=%fused_computation.13 | convolution fusion | flops 50331648 | bytes 1183744 | tf_op jit(solution)/shard_map/dot_general | solution.py:39
  51.6 1.2 convolution_multiply_fusion
  52.8 0.0 copy-start.4
  52.9 0.3 copy.10
  53.2 0.6 reshape.28
  53.8 0.3 copy-done.4
  54.1 0.6 fusion.8
  54.7 2.8 %convolution_multiply_fusion.1 = f32[8,256,16]{1,2,0:T(8,128)S(1)} fusion(f32[8,256,256]{2,1,0:T(8,128)} %fusion.2, f32[8,256,16]{1,2,0:T(8,128)S(1)} %fusion.8), kind=kOutput, calls=%fused_computation.3 | convolution fusion | flops 100696064 | bytes 2359296 | tf_op jit(solution)/shard_map/stk,stq->skq/dot_general | solution.py:46
  57.5 0.3 copy.9
  57.8 0.6 reshape.27
  58.4 0.7 pad_maximum_fusion
  59.2 0.0 all-reduce.4.cloned.1.call-update
  59.2 0.0 all-gather.2.cloned.1.call-start
  59.2 0.5 all-gather.2.cloned.1.call-update
  59.8 19.0 %all-reduce.4.cloned.1.call-done = f32[8,8192]{1,0:T(8,128)} async-done(((f32[8,8192]{1,0:T(8,128)}), f32[8,8192]{1,0:T(8,128)}) %all-reduce.4.cloned.1.call-update) | async-done | bytes 262160 | tf_op jit(solution)/shard_map/psum | solution.py:61
  78.8 0.0 copy-start.3
  78.8 1.2 multiply_reduce_fusion.1
  80.0 38.8 %all-gather.2.cloned.1.call-done = f32[64,8192]{1,0:T(8,128)} async-done(((f32[64,256]{1,0:T(8,128)}), f32[64,8192]{1,0:T(8,128)}) %all-gather.2.cloned.1.call-update) | async-done | bytes 2097168 | tf_op jit(solution)/shard_map/all_gather | solution.py:62
  118.8 0.0 copy-start.2
  118.8 2.0 %multiply_reduce_fusion = f32[64]{0:T(128)S(1)} fusion(f32[64,8192]{1,0:T(8,128)} %all-gather.2.cloned.1.call-done), kind=kLoop, calls=%fused_computation.1 | loop fusion | flops 1048512 | bytes 2097408 | tf_op jit(solution)/shard_map/reduce_sum | solution.py:65
  120.8 0.0 copy-done.3
  120.8 0.2 copy-done.2
  121.0 2.3 %convolution_divide_fusion = f32[8,64]{1,0:T(8,128)} fusion(f32[8,8192]{1,0:T(8,128)S(1)} %copy-done.3, f32[64,8192]{1,0:T(8,128)S(1)} %copy-done.2, f32[64]{0:T(128)S(1)} %add_sqrt_fusion, f32[8]{0:T(128)S(1)} %sqrt_multiply_fusion), kind=kOutput, calls=%fused_computation.4 | convolution fusion | flops 50332672 | bytes 2361632 | tf_op jit(solution)/shard_map/dot_general | solution.py:63
  (2 shorter events, 0.0 us)
Async XLA Ops:
  7.4 8.0 %copy-start = (bf16[128,2048]{1,0:T(8,128)(2,1)S(1)}, bf16[128,2048]{1,0:T(8,128)(2,1)}, u32[]{:S(2)}) copy-start(bf16[128,2048]{1,0:T(8,128)(2,1)} %param.11) | copy-start | bytes 1572868
  7.4 42.5 %all-reduce.6.cloned.1.call-start = ((), (), s32[]{:S(2)}) async-start(), calls=%async_computation.2 | async-start | bytes 4194304 | tf_op jit(solution)/shard_map/psum | solution.py:35
  15.4 6.9 %copy-start.1 = (bf16[2048,2048]{1,0:T(8,128)(2,1)S(1)}, bf16[2048,2048]{1,0:T(8,128)(2,1)}, u32[]{:S(2)}) copy-start(bf16[2048,2048]{1,0:T(8,128)(2,1)} %broadcast_multiply_fusion) | copy-start | bytes 25165828
  15.4 6.9 %copy-start.7 = (bf16[2048,128]{1,0:T(8,128)(2,1)S(1)}, bf16[2048,128]{1,0:T(8,128)(2,1)}, u32[]{:S(2)}) copy-start(bf16[2048,128]{1,0:T(8,128)(2,1)} %param.12) | copy-start | bytes 1572868
  25.7 53.1 %all-reduce.4.cloned.1.call-start = ((), (), s32[]{:S(2)}) async-start(), calls=%async_computation | async-start | bytes 524288 | tf_op jit(solution)/shard_map/psum | solution.py:61
  25.9 6.1 %copy-start.6 = (bf16[2,2048,256]{2,1,0:T(8,128)(2,1)S(1)}, bf16[2,2048,256]{2,1,0:T(8,128)(2,1)}, u32[]{:S(2)}) copy-start(bf16[2,2048,256]{2,1,0:T(8,128)(2,1)} %param.13) | copy-start | bytes 6291460
  32.1 17.8 %copy-start.5 = (bf16[2,128,16]{1,2,0:T(8,128)(2,1)S(1)}, bf16[2,128,16]{1,2,0:T(8,128)(2,1)}, u32[]{:S(2)}) copy-start(bf16[2,128,16]{1,2,0:T(8,128)(2,1)} %param.14) | copy-start | bytes 24580
  52.8 1.2 copy-start.4
  59.2 59.6 %all-gather.2.cloned.1.call-start = ((), (), s32[]{:S(2)}) async-start(), calls=%async_computation.1 | async-start | bytes 2162688 | tf_op jit(solution)/shard_map/all_gather | solution.py:62
  78.8 42.0 %copy-start.3 = (f32[8,8192]{1,0:T(8,128)S(1)}, f32[8,8192]{1,0:T(8,128)}, u32[]{:S(2)}) copy-start(f32[8,8192]{1,0:T(8,128)} %all-reduce.4.cloned.1.call-done) | copy-start | bytes 786436
  118.8 2.2 %copy-start.2 = (f32[64,8192]{1,0:T(8,128)S(1)}, f32[64,8192]{1,0:T(8,128)}, u32[]{:S(2)}) copy-start(f32[64,8192]{1,0:T(8,128)} %all-gather.2.cloned.1.call-done) | copy-start | bytes 6291460
Sparse Core Ops, SparseCore 0:
  25.8 23.9 all-reduce.5
  59.3 19.4 all-reduce.3
Sparse Core Ops, SparseCore 1:
  62.6 56.1 all-gather.1
where the time goes:
time: 131 us
  waiting for transfers between devices  68.3 us (52%)
  matrix products  32.9 us (25%)
  between operations  14.9 us (11%)
  other arithmetic  11.9 us (9%)
  local copies, waits for them, and re-layouts  2.42 us (2%)
    all_gather x1, waiting for transfers between devices, on_device(): every_target = lax.all_gather(targets, ('dp', 'mp'), axis=1, tiled=True)  38.8 us
    psum x1, waiting for transfers between devices, on_device(): features = lax.psum(partial_value, 'mp')  19 us
    psum x1, waiting for transfers between devices, on_device(): lax.psum((down_partial_gradient, up_partial_gradient), 'mp')  9.98 us
    dot_general x1, matrix products, on_device(): jnp.dot(inputs, width_projection[0], preferred_element_type=jnp.float32)  7.79 us
    mul x1, other arithmetic, on_device(): masked_gradient = cotangents * loss_token_mask.astype(jnp.bfloat16)[:, None]  7.23 us
    dot_general x1, matrix products, on_device(): jnp.dot(inputs, adapter_down_weight.T, preferred_element_type=jnp.float32)  6.87 us
    dot_general x1, matrix products, on_device(): jnp.dot(masked_gradient, width_projection[1], preferred_element_type=jnp....  6.11 us
    dot_general x1, matrix products, on_device(): jnp.dot(masked_gradient, adapter_up_weight, preferred_element_type=jnp.fl...  3.41 us
  transfers between devices with their start and end apart: 3, of which 3 were waited for; matrix products, arithmetic and copies ran while one was open for 12% of the time, Pallas kernels for 0%

commit v1 on v0

--- a/solution.py
+++ b/solution.py
@@ -10,6 +10,18 @@
 FEAT = 8192
 adapter_scale = 4.0
 epsilon = 1e-06
+
+
+def collect(value, axis, dim):
+    ways, here = (lax.axis_size(axis), lax.axis_index(axis))
+    grown, reach = (value, 1)
+    while reach < ways:
+        theirs = lax.ppermute(grown, axis, [(d, d ^ reach) for d in range(ways)])
+        mine_first = jnp.concatenate([grown, theirs], axis=dim)
+        theirs_first = jnp.concatenate([theirs, grown], axis=dim)
+        grown = jnp.where(here & reach == 0, mine_first, theirs_first)
+        reach = 2 * reach
+    return grown
 
 
 def on_device(
@@ -59,7 +71,7 @@
         [first_matrix.reshape(samples, KP * KQ), second_matrix.reshape(samples, KP * KQ)], axis=1
     )
     features = lax.psum(partial_value, "mp")
-    every_target = lax.all_gather(targets, ("dp", "mp"), axis=1, tiled=True)
+    every_target = collect(targets, ("dp", "mp"), 1)
     inner = jnp.dot(features, every_target.T, precision=lax.Precision.HIGHEST)
     sample_squares = jnp.sum(features * features, axis=1)
     target_squares = jnp.sum(every_target * every_target, axis=1)

time: 131 us -> 116 us (0.89)
  waiting for transfers between devices: 68.3 us -> 38.2 us
  starting transfers between devices: 0.27 us -> 9.16 us
  matrix products: 32.9 us -> 40.9 us
  between operations: 14.9 us -> 13.5 us
    all_gather x1 -> x0, waiting for transfers between devices: 38.8 us -> none  [on_device(): every_target = lax.all_gather(targets, ('dp', 'mp'), axis=1, tiled=True)]
    ppermute x0 -> x5, waiting for transfers between devices: none -> 38.2 us  [collect(): theirs = lax.ppermute(grown, axis, [(d, d ^ reach) for d in range(ways)])]
    psum x1, waiting for transfers between devices: 19 us -> 0.02 us  [on_device(): features = lax.psum(partial_value, 'mp')]
    psum x1, waiting for transfers between devices: 9.98 us -> 0.01 us  [on_device(): lax.psum((down_partial_gradient, up_partial_gradient), 'mp')]
    ppermute x0 -> x5, starting transfers between devices: none -> 8.93 us  [collect(): theirs = lax.ppermute(grown, axis, [(d, d ^ reach) for d in range(ways)])]
    dot_general x1, matrix products: 3.41 us -> 6.71 us  [on_device(): jnp.dot(masked_gradient, adapter_up_weight, preferred_element_type=jnp.fl...]
    dot_general x1, matrix products: 2.33 us -> 3.99 us  [on_device(): inner = jnp.dot(features, every_target.T, precision=lax.Precision.HIGHEST)]
    dot_general x1, matrix products: 1.21 us -> 2.8 us  [on_device(): jnp.einsum('stk,stq->skq', projected_masked_gradient, compact_down_gradie...]
  transfers between devices with their start and end apart: 3 -> 7, of which waited for: 3 -> 2; matrix products, arithmetic and copies ran while one was open for 12% -> 43% of each run, Pallas kernels for 0% -> 0%
where the time goes in v1:
time: 116 us
  matrix products  40.9 us (35%)
  waiting for transfers between devices  38.2 us (33%)
  between operations  13.5 us (12%)
  other arithmetic  11.9 us (10%)
  starting transfers between devices  9.16 us (8%)
  local copies, waits for them, and re-layouts  1.93 us (2%)
    ppermute x5, waiting for transfers between devices, collect(): theirs = lax.ppermute(grown, axis, [(d, d ^ reach) for d in range(ways)])  38.2 us
    ppermute x5, starting transfers between devices, collect(): theirs = lax.ppermute(grown, axis, [(d, d ^ reach) for d in range(ways)])  8.93 us
    mul x1, other arithmetic, on_device(): masked_gradient = cotangents * loss_token_mask.astype(jnp.bfloat16)[:, None]  7.22 us
    dot_general x1, matrix products, on_device(): jnp.dot(masked_gradient, width_projection[1], preferred_element_type=jnp....  7.09 us
    dot_general x1, matrix products, on_device(): jnp.dot(inputs, width_projection[0], preferred_element_type=jnp.float32)  7.09 us
    dot_general x1, matrix products, on_device(): jnp.dot(inputs, adapter_down_weight.T, preferred_element_type=jnp.float32)  6.84 us
    dot_general x1, matrix products, on_device(): jnp.dot(masked_gradient, adapter_up_weight, preferred_element_type=jnp.fl...  6.71 us
    dot_general x1, matrix products, on_device(): inner = jnp.dot(features, every_target.T, precision=lax.Precision.HIGHEST)  3.99 us
  transfers between devices with their start and end apart: 7, of which 2 were waited for; matrix products, arithmetic and copies ran while one was open for 43% of the time, Pallas kernels for 0%

profile of v1, /device:TPU:0, one launch (start us, length us, event | category | flops | bytes accessed | tf_op | source)
XLA Modules:
  0.0 115.6 jit_solution(12106173265976694086)
XLA Ops:
  6.5 0.0 copy-start
  6.5 0.0 all-reduce.6.cloned.1.call-start
  6.5 0.5 collective-permute-start
  7.0 0.7 convert_element_type.2
  7.7 7.2 %broadcast_multiply_fusion = bf16[2048,2048]{1,0:T(8,128)(2,1)} fusion(bf16[2048,2048]{1,0:T(8,128)(2,1)} %param.9, bf16[2048]{0:T(1024)(128)(2,1)S(1)} %convert_element_type.2), kind=kLoop, calls=%fused_computation | loop fusion | flops 4194304 | bytes 16781312 | tf_op jit(solution)/shard_map/mul | solution.py:38
  14.9 0.0 copy-done
  14.9 0.0 copy-start.1
  14.9 0.0 copy-start.4
  14.9 6.8 %fusion.17 = f32[2048,128]{1,0:T(8,128)} fusion(bf16[2048,2048]{1,0:T(8,128)(2,1)} %param.8, bf16[128,2048]{1,0:T(8,128)(2,1)S(1)} %copy-done), kind=kOutput, calls=%fused_computation.30 | convolution fusion | flops 1073741824 | bytes 9961472 | tf_op jit(solution)/shard_map/dot_general | solution.py:41
  21.8 0.0 collective-permute-done
  21.8 0.0 copy-done.1
  21.8 2.6 %collective-permute-start.1 = (f32[64,512]{1,0:T(8,128)S(1)}, f32[64,512]{1,0:T(8,128)S(1)}, u32[]{:S(2)}, u32[]{:S(2)}) collective-permute-start(f32[64,512]{1,0:T(8,128)S(1)} %maximum_select_fusion.7), channel_id=1, source_target_pairs={{0,2},{1,3},{2,0},{3,1},{4,6},{5,7},{6,4},{7,5},{8,10},{9,11},{10,... | collective-permute-start | bytes 393224 | tf_op jit(solution)/shard_map/ppermute | solution.py:19
  24.4 0.0 copy-done.4
  24.4 6.7 %fusion.16 = f32[2048,128]{1,0:T(8,128)} fusion(bf16[2048,2048]{1,0:T(8,128)(2,1)} %broadcast_multiply_fusion, bf16[2048,128]{1,0:T(8,128)(2,1)S(1)} %copy-done.4), kind=kOutput, calls=%fused_computation.29 | convolution fusion | flops 1073741824 | bytes 9961472 | tf_op jit(solution)/shard_map/dot_general | solution.py:44
  31.1 0.0 copy-start.3
  31.1 0.0 all-reduce.6.cloned.1.call-update
  31.1 0.2 all-reduce.4.cloned.1.call-start
  31.4 0.0 collective-permute-done.1
  31.4 1.6 %collective-permute-start.2 = (f32[64,1024]{1,0:T(8,128)S(1)}, f32[64,1024]{1,0:T(8,128)S(1)}, u32[]{:S(2)}, u32[]{:S(2)}) collective-permute-start(f32[64,1024]{1,0:T(8,128)S(1)} %maximum_select_fusion.6), channel_id=1, source_target_pairs={{0,4},{1,5},{2,6},{3,7},{4,0},{5,1},{6,2},{7,3},{8,12},{9,13},{10,... | collective-permute-start | bytes 786440 | tf_op jit(solution)/shard_map/ppermute | solution.py:19
  33.0 0.0 copy-done.3
  33.0 7.1 %fusion.2 = f32[8,256,256]{2,1,0:T(8,128)} fusion(bf16[8,256,2048]{2,1,0:T(8,128)(2,1)} %bitcast.33, bf16[2,2048,256]{2,1,0:T(8,128)(2,1)S(1)} %copy-done.3), kind=kOutput, calls=%fused_computation.8 | convolution fusion | flops 2147483648 | bytes 11534336 | tf_op jit(solution)/shard_map/dot_general | solution.py:55
  40.1 0.0 collective-permute-done.2
  40.1 1.6 %collective-permute-start.3 = (f32[64,2048]{1,0:T(8,128)S(1)}, f32[64,2048]{1,0:T(8,128)S(1)}, u32[]{:S(2)}, u32[]{:S(2)}) collective-permute-start(f32[64,2048]{1,0:T(8,128)S(1)} %maximum_select_fusion.5), channel_id=1, source_target_pairs={{0,8},{1,9},{2,10},{3,11},{4,12},{5,13},{6,14},{7,15},{8,0},{9,1},... | collective-permute-start | bytes 1572872 | tf_op jit(solution)/shard_map/ppermute | solution.py:19
  41.8 7.1 %fusion.4 = f32[8,256,256]{2,1,0:T(8,128)} fusion(bf16[8,256,2048]{2,1,0:T(8,128)(2,1)} %bitcast.36, bf16[2,2048,256]{2,1,0:T(8,128)(2,1)S(1)} %copy-done.3), kind=kOutput, calls=%fused_computation.10 | convolution fusion | flops 2147483648 | bytes 11534336 | tf_op jit(solution)/shard_map/dot_general | solution.py:52
  48.9 0.0 copy-start.2
  48.9 5.1 %collective-permute-done.3 = f32[64,2048]{1,0:T(8,128)S(1)} collective-permute-done((f32[64,2048]{1,0:T(8,128)S(1)}, f32[64,2048]{1,0:T(8,128)S(1)}, u32[]{:S(2)}, u32[]{:S(2)}) %collective-permute-start.3) | collective-permute-done | bytes 524320 | tf_op jit(solution)/shard_map/ppermute | solution.py:19
  53.9 0.1 maximum_select_fusion.4
  54.1 2.6 %collective-permute-start.4 = (f32[64,4096]{1,0:T(8,128)S(1)}, f32[64,4096]{1,0:T(8,128)}, u32[]{:S(2)}, u32[]{:S(2)}) collective-permute-start(f32[64,4096]{1,0:T(8,128)S(1)} %maximum_select_fusion.4), channel_id=1, source_target_pairs={{0,16},{1,17},{2,18},{3,19},{4,20},{5,21},{6,22},{7,23},{8,24},{9,... | collective-permute-start | bytes 3145736 | tf_op jit(solution)/shard_map/ppermute | solution.py:19
  56.7 0.0 all-reduce.6.cloned.1.call-done
  56.7 0.0 copy-done.2
  56.7 1.8 %fusion.9 = f32[8,256,16]{1,2,0:T(8,128)S(1)} fusion(f32[8,256,128]{2,1,0:T(8,128)} %get-tuple-element.5, bf16[2,128,16]{1,2,0:T(8,128)(2,1)S(1)} %copy-done.2), kind=kOutput, calls=%fused_computation.20 | convolution fusion | flops 50331648 | bytes 1183744 | tf_op jit(solution)/shard_map/dot_general | solution.py:51
  58.5 2.8 %convolution_multiply_fusion = f32[8,256,16]{1,2,0:T(8,128)S(1)} fusion(f32[8,256,256]{2,1,0:T(8,128)} %fusion.2, f32[8,256,16]{1,2,0:T(8,128)S(1)} %fusion.9), kind=kOutput, calls=%fused_computation.4 | convolution fusion | flops 100696064 | bytes 2359296 | tf_op jit(solution)/shard_map/stk,stq->skq/dot_general | solution.py:64
  61.3 0.3 copy.10
  61.7 0.6 reshape.28
  62.3 1.8 %fusion.11 = f32[8,256,16]{1,2,0:T(8,128)S(1)} fusion(f32[8,256,128]{2,1,0:T(8,128)} %get-tuple-element.6, bf16[2,128,16]{1,2,0:T(8,128)(2,1)S(1)} %copy-done.2), kind=kOutput, calls=%fused_computation.22 | convolution fusion | flops 50331648 | bytes 1183744 | tf_op jit(solution)/shard_map/dot_general | solution.py:50
  64.1 2.8 %convolution_multiply_fusion.1 = f32[8,256,16]{1,2,0:T(8,128)S(1)} fusion(f32[8,256,256]{2,1,0:T(8,128)} %fusion.4, f32[8,256,16]{1,2,0:T(8,128)S(1)} %fusion.11), kind=kOutput, calls=%fused_computation.5 | convolution fusion | flops 100696064 | bytes 2359296 | tf_op jit(solution)/shard_map/stk,stq->skq/dot_general | solution.py:58
  66.9 0.3 copy.9
  67.2 0.6 reshape.27
  67.9 0.7 pad_maximum_fusion
  68.6 0.0 all-reduce.4.cloned.1.call-update
  68.6 33.1 %collective-permute-done.4 = f32[64,4096]{1,0:T(8,128)} collective-permute-done((f32[64,4096]{1,0:T(8,128)S(1)}, f32[64,4096]{1,0:T(8,128)}, u32[]{:S(2)}, u32[]{:S(2)}) %collective-permute-start.4) | collective-permute-done | bytes 1048608 | tf_op jit(solution)/shard_map/ppermute | solution.py:19
  101.7 1.9 %multiply_reduce_fusion = f32[64]{0:T(128)S(1)} fusion(f32[64,4096]{1,0:T(8,128)S(1)} %maximum_select_fusion.4, f32[64,4096]{1,0:T(8,128)} %collective-permute-done.4, pred[]{:T(512)S(6)} %eq.15), kind=kLoop, calls=%fused_computation.2 | loop fusion | flops 2621376 | bytes 2097409 | tf_op jit(solution)/shard_map/reduce_sum | solution.py:77
  103.6 0.0 all-reduce.4.cloned.1.call-done
  103.7 1.1 multiply_reduce_fusion.1
  104.8 4.0 %fusion.1 = f32[8,64]{1,0:T(8,128)} fusion(f32[8,8192]{1,0:T(8,128)} %all-reduce.4.cloned.1.call-done, f32[64,4096]{1,0:T(8,128)} %collective-permute-done.4, f32[64,4096]{1,0:T(8,128)S(1)} %maximum_select_fusion.4, pred[]{:T(512)S(6)} %eq.15, f32[64]{0:T(128)S(1)} %add_sqrt_fusion, f32[8]{0:T(128)S(1)} %sqrt_multiply_fusion), kind=kOutput, calls=%fused_computation.6 | convolution fusion | flops 51905536 | bytes 2361633 | tf_op jit(solution)/shard_map/dot_general | solution.py:75
  (5 shorter events, 0.1 us)
Async XLA Ops:
  6.5 8.4 %copy-start = (bf16[128,2048]{1,0:T(8,128)(2,1)S(1)}, bf16[128,2048]{1,0:T(8,128)(2,1)}, u32[]{:S(2)}) copy-start(bf16[128,2048]{1,0:T(8,128)(2,1)} %param.11) | copy-start | bytes 1572868
  6.5 50.2 %all-reduce.6.cloned.1.call-start = ((), (), s32[]{:S(2)}) async-start(), calls=%async_computation.1 | async-start | bytes 4194304 | tf_op jit(solution)/shard_map/psum | solution.py:47
  6.5 15.2 %collective-permute-start = (f32[64,256]{1,0:T(8,128)}, f32[64,256]{1,0:T(8,128)S(1)}, u32[]{:S(2)}, u32[]{:S(2)}) collective-permute-start(f32[64,256]{1,0:T(8,128)} %param.15), channel_id=1, source_target_pairs={{0,1},{1,0},{2,3},{3,2},{4,5},{5,4},{6,7},{7,6},{8,9},{9,8},{10,11... | collective-permute-start | bytes 196616 | tf_op jit(solution)/shard_map/ppermute | solution.py:19
  14.9 6.9 %copy-start.1 = (f32[64,256]{1,0:T(8,128)S(1)}, f32[64,256]{1,0:T(8,128)}, u32[]{:S(2)}) copy-start(f32[64,256]{1,0:T(8,128)} %param.15) | copy-start | bytes 196612
  14.9 9.5 %copy-start.4 = (bf16[2048,128]{1,0:T(8,128)(2,1)S(1)}, bf16[2048,128]{1,0:T(8,128)(2,1)}, u32[]{:S(2)}) copy-start(bf16[2048,128]{1,0:T(8,128)(2,1)} %param.12) | copy-start | bytes 1572868
  21.8 9.6 %collective-permute-start.1 = (f32[64,512]{1,0:T(8,128)S(1)}, f32[64,512]{1,0:T(8,128)S(1)}, u32[]{:S(2)}, u32[]{:S(2)}) collective-permute-start(f32[64,512]{1,0:T(8,128)S(1)} %maximum_select_fusion.7), channel_id=1, source_target_pairs={{0,2},{1,3},{2,0},{3,1},{4,6},{5,7},{6,4},{7,5},{8,10},{9,11},{10,... | collective-permute-start | bytes 393224 | tf_op jit(solution)/shard_map/ppermute | solution.py:19
  31.1 1.9 %copy-start.3 = (bf16[2,2048,256]{2,1,0:T(8,128)(2,1)S(1)}, bf16[2,2048,256]{2,1,0:T(8,128)(2,1)}, u32[]{:S(2)}) copy-start(bf16[2,2048,256]{2,1,0:T(8,128)(2,1)} %param.13) | copy-start | bytes 6291460
  31.1 72.5 %all-reduce.4.cloned.1.call-start = ((), (), s32[]{:S(2)}) async-start(), calls=%async_computation | async-start | bytes 524288 | tf_op jit(solution)/shard_map/psum | solution.py:73
  31.4 8.7 %collective-permute-start.2 = (f32[64,1024]{1,0:T(8,128)S(1)}, f32[64,1024]{1,0:T(8,128)S(1)}, u32[]{:S(2)}, u32[]{:S(2)}) collective-permute-start(f32[64,1024]{1,0:T(8,128)S(1)} %maximum_select_fusion.6), channel_id=1, source_target_pairs={{0,4},{1,5},{2,6},{3,7},{4,0},{5,1},{6,2},{7,3},{8,12},{9,13},{10,... | collective-permute-start | bytes 786440 | tf_op jit(solution)/shard_map/ppermute | solution.py:19
  40.1 13.8 %collective-permute-start.3 = (f32[64,2048]{1,0:T(8,128)S(1)}, f32[64,2048]{1,0:T(8,128)S(1)}, u32[]{:S(2)}, u32[]{:S(2)}) collective-permute-start(f32[64,2048]{1,0:T(8,128)S(1)} %maximum_select_fusion.5), channel_id=1, source_target_pairs={{0,8},{1,9},{2,10},{3,11},{4,12},{5,13},{6,14},{7,15},{8,0},{9,1},... | collective-permute-start | bytes 1572872 | tf_op jit(solution)/shard_map/ppermute | solution.py:19
  48.9 7.9 %copy-start.2 = (bf16[2,128,16]{1,2,0:T(8,128)(2,1)S(1)}, bf16[2,128,16]{1,2,0:T(8,128)(2,1)}, u32[]{:S(2)}) copy-start(bf16[2,128,16]{1,2,0:T(8,128)(2,1)} %param.14) | copy-start | bytes 24580
  54.1 47.6 %collective-permute-start.4 = (f32[64,4096]{1,0:T(8,128)S(1)}, f32[64,4096]{1,0:T(8,128)}, u32[]{:S(2)}, u32[]{:S(2)}) collective-permute-start(f32[64,4096]{1,0:T(8,128)S(1)} %maximum_select_fusion.4), channel_id=1, source_target_pairs={{0,16},{1,17},{2,18},{3,19},{4,20},{5,21},{6,22},{7,23},{8,24},{9,... | collective-permute-start | bytes 3145736 | tf_op jit(solution)/shard_map/ppermute | solution.py:19
Sparse Core Ops, SparseCore 0:
  31.3 21.6 all-reduce.5
  68.7 16.5 all-reduce.3
